TPU v7x, 128 devices: a whole 4x4x4 slice. The times are simulated.
128 devices in a mesh: pts: 8 (over x, core), snap: 16 (over z, y).
Axes of the slice: x: 4, y: 4, z: 4, core: 2. Of those that a mesh axis runs over, the one named last changes fastest.
Arguments:
- snapshots: bfloat16 [1024, 3, 65536], P('snap', None, 'pts')
- block_starts: int32 [31], replicated, may hold values from 0 to 960, as said below
- point_slab: int32 [65536], P(('pts', 'snap')), may hold values from 0 to 15
- slab_weight: float32 [16], replicated, may hold values from 1 to 10
Outputs:
- mode_field: bfloat16 [2, 33, 31, 3, 65536], P(None, None, None, None, ('pts', 'snap'))
- r_factor: float32 [2, 33, 31, 31], replicated
Inputs may be any that keep to these rules, and one draw needn't show every extreme that they name: `block_starts`: strictly increasing; the first is 0 and the last is 960; neighbours lie more than 16 apart.
All inputs are finite; a program needn't handle non-finite values.
Results may differ from a plain program's by a relative error of at most 0.0017.
The roundings to bfloat16 on the way count: a program that leaves them out, or rounds other values in their place, can miss the bound.
Values may be sent and summed in bfloat16 or wider, within the bound.
No kernel may reach another device: no remote copies, remote signals or barrier semaphores. Data moves between devices by JAX's collectives and lax.ppermute only.
A program may use at most 128 MiB of HBM per device.

v0:
```python
import math
import jax
import jax.numpy as jnp
from jax import lax
from jax.sharding import PartitionSpec as P

NT = 1024
WIN = 64


def make_tables(length, freq_count):
    steps_time = jnp.arange(length, dtype=jnp.int32)
    freq_index = jnp.arange(freq_count, dtype=jnp.int32)
    phase_index = freq_index[:, None] * steps_time[None, :] % length
    angle_value = 2.0 * math.pi / length * phase_index.astype(jnp.float32)
    window = 0.5 - 0.5 * jnp.cos(2.0 * math.pi / length * steps_time.astype(jnp.float32))
    dft_table = jnp.stack(
        [window[None, :] * jnp.cos(angle_value), -window[None, :] * jnp.sin(angle_value)]
    ).astype(jnp.bfloat16)
    row_sums = jnp.sum(dft_table.astype(jnp.float32), axis=2)
    return (dft_table, row_sums)


def spectra(series, starts, dft_table, row_sums):
    blocks = jax.vmap(lambda offset: lax.dynamic_slice_in_dim(series, offset, WIN, 0))(starts)
    raw_spec = jnp.einsum("kfw,bwcp->kfbcp", dft_table, blocks, preferred_element_type=jnp.float32)
    time_mean = jnp.sum(series.astype(jnp.float32), axis=0) / NT
    return raw_spec - row_sums[:, :, None, None, None] * time_mean[None, None, None]


def gram(amplitude):
    highest = lax.Precision.HIGHEST
    amp_real, amp_imag = (amplitude[0], amplitude[1])
    part_real = jnp.einsum("fbn,fdn->bdf", amp_real, amp_real, precision=highest) + jnp.einsum(
        "fbn,fdn->bdf", amp_imag, amp_imag, precision=highest
    )
    part_imag = jnp.einsum("fbn,fdn->bdf", amp_real, amp_imag, precision=highest) - jnp.einsum(
        "fbn,fdn->bdf", amp_imag, amp_real, precision=highest
    )
    return (part_real, part_imag)


def complex_cholesky(gram_real, gram_imag):
    size_n = gram_real.shape[0]
    positions = jnp.arange(size_n, dtype=jnp.int32)
    rows_real = []
    rows_imag = []
    for column in range(size_n):
        rest_real = gram_real[column]
        rest_imag = gram_imag[column]
        if column > 0:
            done_real = jnp.stack(rows_real)
            done_imag = jnp.stack(rows_imag)
            above_real = done_real[:, column]
            above_imag = done_imag[:, column]
            rest_real = rest_real - jnp.sum(
                above_real[:, None] * done_real + above_imag[:, None] * done_imag, axis=0
            )
            rest_imag = rest_imag - jnp.sum(
                above_real[:, None] * done_imag - above_imag[:, None] * done_real, axis=0
            )
        pivot_value = jnp.sqrt(rest_real[column])
        keep_real = (positions >= column)[:, None]
        keep_imag = (positions > column)[:, None]
        rows_real.append(jnp.where(keep_real, rest_real / pivot_value, jnp.zeros_like(rest_real)))
        rows_imag.append(jnp.where(keep_imag, rest_imag / pivot_value, jnp.zeros_like(rest_imag)))
    return (jnp.stack(rows_real), jnp.stack(rows_imag))


def upper_inverse(upper_real, upper_imag):
    size_n = upper_real.shape[0]
    identity = jnp.eye(size_n, dtype=upper_real.dtype)
    rows_real = []
    rows_imag = []
    for row_index in reversed(range(size_n)):
        rest_real = jnp.broadcast_to(identity[row_index][:, None], upper_real.shape[1:])
        rest_imag = jnp.zeros_like(rest_real)
        if row_index < size_n - 1:
            done_real = jnp.stack(rows_real[::-1])
            done_imag = jnp.stack(rows_imag[::-1])
            coef_real = upper_real[row_index, row_index + 1 :]
            coef_imag = upper_imag[row_index, row_index + 1 :]
            rest_real = rest_real - jnp.sum(
                coef_real[:, None] * done_real - coef_imag[:, None] * done_imag, axis=0
            )
            rest_imag = rest_imag - jnp.sum(
                coef_real[:, None] * done_imag + coef_imag[:, None] * done_real, axis=0
            )
        pivot_value = upper_real[row_index, row_index]
        rows_real.append(rest_real / pivot_value)
        rows_imag.append(rest_imag / pivot_value)
    return (jnp.stack(rows_real[::-1]), jnp.stack(rows_imag[::-1]))


def project(amplitude, inv_real, inv_imag):
    highest = lax.Precision.HIGHEST
    amp_real, amp_imag = (amplitude[0], amplitude[1])
    mode_real = jnp.einsum("fbn,bmf->fmn", amp_real, inv_real, precision=highest) - jnp.einsum(
        "fbn,bmf->fmn", amp_imag, inv_imag, precision=highest
    )
    mode_imag = jnp.einsum("fbn,bmf->fmn", amp_real, inv_imag, precision=highest) + jnp.einsum(
        "fbn,bmf->fmn", amp_imag, inv_real, precision=highest
    )
    return jnp.stack([mode_real, mode_imag])


def on_device(snapshots, block_starts, point_slab, slab_weight):
    dft_table, row_sums = make_tables(WIN, WIN // 2 + 1)
    series = lax.all_to_all(snapshots, "snap", split_axis=2, concat_axis=0, tiled=True)
    spectrum = spectra(series, block_starts, dft_table, row_sums)
    freq_count = spectrum.shape[1]
    block_count = spectrum.shape[2]
    points = spectrum.shape[4]
    all_points = points * lax.axis_size("pts") * lax.axis_size("snap")
    slab_ids = jnp.arange(slab_weight.shape[0], dtype=jnp.int32)
    one_hot = (point_slab[:, None] == slab_ids[None, :]).astype(jnp.float32)
    weights = jnp.dot(one_hot, slab_weight, precision=lax.Precision.HIGHEST)
    root_weight = jnp.sqrt(weights / (0.375 * WIN))
    amplitude = (spectrum * root_weight).reshape(2, freq_count, block_count, 3 * points)
    part_real, part_imag = gram(amplitude)
    norm_scale = 1.0 / (3.0 * all_points)
    sum_real, sum_imag = lax.psum((part_real, part_imag), ("pts", "snap"))
    upper_real, upper_imag = complex_cholesky(sum_real * norm_scale, sum_imag * norm_scale)
    inv_real, inv_imag = upper_inverse(upper_real, upper_imag)
    mode_field = (
        project(amplitude, inv_real, inv_imag)
        .reshape(2, freq_count, block_count, 3, points)
        .astype(jnp.bfloat16)
    )
    r_factor = jnp.transpose(jnp.stack([upper_real, upper_imag]), (0, 3, 1, 2))
    return (mode_field, r_factor)


def solution(mesh):
    in_specs = (P("snap", None, "pts"), P(), P(("pts", "snap")), P())
    out_specs = (P(None, None, None, None, ("pts", "snap")), P())
    return jax.shard_map(
        on_device, mesh=mesh, in_specs=in_specs, out_specs=out_specs, check_vma=False
    )
```

profile of v0, /device:TPU:1, one launch (start us, length us, event | category | flops | bytes accessed | tf_op | source)
XLA Modules:
  0.0 542.6 jit_solution(6044256804985214735)
XLA Ops:
  7.2 11.3 %copy.17234 = bf16[64,3,8192]{0,1,2:T(4,128)(2,1)} copy(bf16[64,3,8192]{2,0,1:T(8,128)(2,1)} %param.4) | data formatting | bytes 6291456 | tf_op args[0]
  18.4 13.4 %reshape.4626 = bf16[16,2,49152]{2,1,0:T(2,128)(2,1)} reshape(bf16[8192,3,64]{2,1,0:T(4,128)(2,1)} %bitcast.635) | data formatting | bytes 6291456
  31.8 8.6 %all-to-all-start = ((bf16[16,2,49152]{2,1,0:T(2,128)(2,1)}), bf16[16,2,49152]{2,1,0:T(2,128)(2,1)S(1)}, u32[]{:S(2)}, u32[]{:S(2)}) async-start(bf16[16,2,49152]{2,1,0:T(2,128)(2,1)} %reshape.4626), calls=%async_computation | async-start | bytes 6291456 | tf_op jit(solution)/shard_map/all_to_all | solution.py:109
  41.5 45.5 %all-to-all-done = bf16[16,2,49152]{2,1,0:T(2,128)(2,1)S(1)} async-done(((bf16[16,2,49152]{2,1,0:T(2,128)(2,1)}), bf16[16,2,49152]{2,1,0:T(2,128)(2,1)S(1)}, u32[]{:S(2)}, u32[]{:S(2)}) %all-to-all-start) | async-done | bytes 3145760 | tf_op jit(solution)/shard_map/all_to_all | solution.py:109
  87.0 9.3 %reshape.4627 = bf16[8192,3,64]{2,1,0:T(4,128)(2,1)} reshape(bf16[16,2,49152]{2,1,0:T(2,128)(2,1)S(1)} %all-to-all-done) | data formatting | bytes 6291456
  96.3 8.3 %copy.17846 = bf16[64,3,16,512]{3,2,0,1:T(8,128)(2,1)S(1)} copy(bf16[64,3,16,512]{0,1,3,2:T(4,128)(2,1)} %bitcast.634) | data formatting | bytes 6291456 | tf_op jit(solution)/shard_map/all_to_all | solution.py:109
  104.6 0.8 convert_reduce_fusion
  105.4 4.7 copy.17236
  110.2 11.5 %gather_fusion = bf16[31,64,3,512]{3,2,1,0:T(4,128)(2,1)} fusion(bf16[1024,3,512]{2,1,0:T(4,128)(2,1)} %bitcast.633, s32[31]{0:T(128)S(1)} %fusion.108), kind=kCustom, calls=%fused_computation | custom fusion | bytes 12190068 | tf_op jit(solution)/shard_map/vmap()/gather | solution.py:25
  121.7 11.4 %subtract_multiply_fusion = f32[2,33,31,3,512]{4,1,3,2,0:T(8,128)} fusion(f32[512]{0:T(512)S(1)} %multiply_sqrt_fusion, f32[2,33,3,512]{3,1,2,0:T(8,128)S(1)} %broadcast_multiply_fusion.2, bf16[31,64,3,512]{3,2,1,0:T(4,128)(2,1)} %gather_fusion, bf16[1,33,64]{2,1,0:T(8,128)(2,1)S(1)} %get-tuple-element.379, bf16[1,33,64]{2,1,0:T(8,128)(2,1)S(1)} %get-tuple-element.380), kind=kOutput, calls=%fused_computation.1 | convolution fusion | flops 408562176 | bytes 19081472 | tf_op jit(solution)/shard_map/kfw,bwcp->kfbcp/dot_general | solution.py:26
  133.2 12.5 %fusion.116 = (f32[1,33,31,3,512]{4,1,3,2,0:T(8,128)}, f32[1,33,31,3,512]{4,1,3,2,0:T(8,128)}) fusion(f32[2,33,31,3,512]{4,1,3,2,0:T(8,128)} %subtract_multiply_fusion), kind=kLoop, calls=%fused_computation.928 | loop fusion | bytes 25141248 | tf_op jit(solution)/shard_map/slice | solution.py:33
  145.7 10.7 %copy.17238 = f32[1,33,31,3,512]{4,3,2,1,0:T(4,128)} copy(f32[1,33,31,3,512]{4,1,3,2,0:T(8,128)} %get-tuple-element.190) | data formatting | bytes 12570624 | tf_op jit(solution)/shard_map/slice | solution.py:33
  156.4 11.6 %squeeze.62 = f32[33,31,1536]{2,1,0:T(8,128)} reshape(f32[1,33,31,3,512]{4,3,2,1,0:T(4,128)} %copy.17238) | data formatting | bytes 12570624 | tf_op jit(solution)/shard_map/squeeze | solution.py:33
  168.0 10.7 %copy.17239 = f32[1,33,31,3,512]{4,3,2,1,0:T(4,128)} copy(f32[1,33,31,3,512]{4,1,3,2,0:T(8,128)} %get-tuple-element.191) | data formatting | bytes 12570624 | tf_op jit(solution)/shard_map/slice | solution.py:33
  178.7 11.4 %squeeze.63 = f32[33,31,1536]{2,1,0:T(8,128)} reshape(f32[1,33,31,3,512]{4,3,2,1,0:T(4,128)} %copy.17239) | data formatting | bytes 12570624 | tf_op jit(solution)/shard_map/squeeze | solution.py:33
  190.1 9.6 %fusion.123 = f32[33,31,31]{2,1,0:T(8,128)S(1)} fusion(f32[33,31,1536]{2,1,0:T(8,128)} %squeeze.62, f32[33,31,1536]{2,1,0:T(8,128)} %squeeze.63), kind=kOutput, calls=%fused_computation.935 | convolution fusion | flops 584534016 | bytes 12697476 | tf_op jit(solution)/shard_map/fbn,fdn->bdf/dot_general | solution.py:37
  199.8 6.0 %fusion.122 = f32[33,31,31]{2,1,0:T(8,128)S(1)} fusion(f32[33,31,1536]{2,1,0:T(8,128)S(1)} %copy-done.3, f32[33,31,1536]{2,1,0:T(8,128)S(1)} %copy-done.2), kind=kOutput, calls=%fused_computation.934 | convolution fusion | flops 584534016 | bytes 12697476 | tf_op jit(solution)/shard_map/fbn,fdn->bdf/dot_general | solution.py:37
  205.7 6.3 %fusion.120 = f32[33,31,31]{2,1,0:T(8,128)S(1)} fusion(f32[33,31,1536]{2,1,0:T(8,128)S(1)} %copy-done.2), kind=kOutput, calls=%fused_computation.932 | convolution fusion | flops 584534016 | bytes 6412164 | tf_op jit(solution)/shard_map/fbn,fdn->bdf/dot_general | solution.py:34
  212.1 6.1 %fusion.121 = f32[33,31,31]{2,1,0:T(8,128)S(1)} fusion(f32[33,31,1536]{2,1,0:T(8,128)S(1)} %copy-done.3), kind=kOutput, calls=%fused_computation.933 | convolution fusion | flops 584534016 | bytes 6412164 | tf_op jit(solution)/shard_map/fbn,fdn->bdf/dot_general | solution.py:34
  220.1 0.9 subtract_bitcast_fusion
  221.0 0.9 add_bitcast_fusion
  221.9 147.2 %all-reduce.4.cloned.1.call-done = (f32[31,31,33]{2,0,1:T(8,128)}, f32[31,31,33]{2,0,1:T(8,128)}) async-done(((f32[31,31,33]{2,0,1:T(8,128)}, f32[31,31,33]{2,0,1:T(8,128)}), (f32[31,31,33]{2,0,1:T(8,128)}, f32[31,31,33]{2,0,1:T(8,128)})) %all-reduce.4.cloned.1.call-update) | async-done | bytes 253720 | tf_op jit(solution)/shard_map/psum | solution.py:122
  369.1 1.1 broadcast_multiply_fusion.1
  370.2 1.1 broadcast_multiply_fusion
  395.6 0.8 stack.292
  412.3 0.8 stack.308
  419.7 0.7 stack.314
  420.4 0.7 stack.315
  422.2 0.7 stack.317
  422.9 0.7 stack.316
  424.7 0.8 stack.383
  427.1 0.8 stack.385
  427.9 1.0 copy.17842
  429.0 2.0 copy.17844
  460.8 0.9 stack.375
  461.7 0.7 stack.374
  463.0 0.7 stack.376
  463.7 0.7 stack.377
  465.0 0.8 stack.378
  466.4 9.6 %fusion.124 = f32[33,31,1536]{2,1,0:T(8,128)} fusion(f32[31,31,33]{0,1,2:T(8,128)S(1)} %copy.17831, f32[33,31,1536]{2,1,0:T(8,128)} %squeeze.62), kind=kOutput, calls=%fused_computation.936 | convolution fusion | flops 584534016 | bytes 12697476 | tf_op jit(solution)/shard_map/fbn,bmf->fmn/dot_general | solution.py:98
  476.1 0.8 stack.379
  477.5 9.6 %fusion.125 = f32[33,31,1536]{2,1,0:T(8,128)} fusion(f32[31,31,33]{0,1,2:T(8,128)S(1)} %copy.17835, f32[33,31,1536]{2,1,0:T(8,128)} %squeeze.62), kind=kOutput, calls=%fused_computation.937 | convolution fusion | flops 584534016 | bytes 12697476 | tf_op jit(solution)/shard_map/fbn,bmf->fmn/dot_general | solution.py:101
  487.0 9.6 %subtract_convert_fusion = bf16[33,31,1536]{2,1,0:T(8,128)(2,1)} fusion(f32[33,31,1536]{2,1,0:T(8,128)S(1)} %bitcast.638, f32[31,31,33]{0,1,2:T(8,128)S(1)} %copy.17835, f32[33,31,1536]{2,1,0:T(8,128)} %squeeze.63), kind=kOutput, calls=%fused_computation.4 | convolution fusion | flops 587676672 | bytes 15840132 | tf_op jit(solution)/shard_map/fbn,bmf->fmn/dot_general | solution.py:98
  496.6 8.7 %stack.380 = bf16[1,33,31,3,512]{4,3,2,1,0:T(4,128)(2,1)} reshape(bf16[33,31,1536]{2,1,0:T(8,128)(2,1)} %subtract_convert_fusion) | data formatting | bytes 6285312 | tf_op jit(solution)/shard_map/stack | solution.py:104
  505.3 8.9 %add_convert_fusion = bf16[33,31,1536]{2,1,0:T(8,128)(2,1)S(1)} fusion(f32[33,31,1536]{2,1,0:T(8,128)} %fusion.125, f32[31,31,33]{0,1,2:T(8,128)} %copy-done.5, f32[33,31,1536]{2,1,0:T(8,128)} %squeeze.63), kind=kOutput, calls=%fused_computation.3 | convolution fusion | flops 587676672 | bytes 15840132 | tf_op jit(solution)/shard_map/fbn,bmf->fmn/dot_general | solution.py:101
  514.2 5.8 %stack.381 = bf16[1,33,31,3,512]{4,3,2,1,0:T(4,128)(2,1)} reshape(bf16[33,31,1536]{2,1,0:T(8,128)(2,1)S(1)} %add_convert_fusion) | data formatting | bytes 6285312 | tf_op jit(solution)/shard_map/stack | solution.py:104
  520.0 7.6 %pad_maximum_fusion = bf16[2,33,31,3,512]{4,3,2,1,0:T(4,128)(2,1)S(1)} fusion(bf16[1,33,31,3,512]{4,3,2,1,0:T(4,128)(2,1)} %stack.381, bf16[1,33,31,3,512]{4,3,2,1,0:T(4,128)(2,1)} %stack.380), kind=kLoop, calls=%fused_computation.2 | loop fusion | flops 3142656 | bytes 12570624 | tf_op jit(solution)/shard_map/stack | solution.py:104
  527.7 7.6 %copy.17843 = bf16[2,33,31,3,512]{4,0,3,2,1:T(2,128)(2,1)} copy(bf16[2,33,31,3,512]{4,3,2,1,0:T(4,128)(2,1)S(1)} %pad_maximum_fusion) | data formatting | bytes 12570624
  (954 shorter events, 81.2 us)
Async XLA Ops:
  7.2 34.0 %copy-start = (f32[16]{0:T(128)S(1)}, f32[16]{0:T(128)}, u32[]{:S(2)}) copy-start(f32[16]{0:T(128)} %param.7) | copy-start | bytes 196
  18.4 22.7 %copy-start.7 = (s32[31]{0:T(128)S(1)}, s32[31]{0:T(128)}, u32[]{:S(2)}) copy-start(s32[31]{0:T(128)} %param.5) | copy-start | bytes 376
  18.4 22.7 %copy-start.6 = (s32[512]{0:T(512)S(1)}, s32[512]{0:T(512)}, u32[]{:S(2)}) copy-start(s32[512]{0:T(512)} %param.6) | copy-start | bytes 6148
  31.8 55.2 %all-to-all-start = ((bf16[16,2,49152]{2,1,0:T(2,128)(2,1)}), bf16[16,2,49152]{2,1,0:T(2,128)(2,1)S(1)}, u32[]{:S(2)}, u32[]{:S(2)}) async-start(bf16[16,2,49152]{2,1,0:T(2,128)(2,1)} %reshape.4626), calls=%async_computation | async-start | bytes 6291456 | tf_op jit(solution)/shard_map/all_to_all | solution.py:109
  40.4 328.7 %all-reduce.4.cloned.1.call-start = ((), (), s32[]{:S(2)}) async-start(), calls=%async_computation.1 | async-start | bytes 2031616 | tf_op jit(solution)/shard_map/psum | solution.py:122
  190.1 9.6 %copy-start.2 = (f32[33,31,1536]{2,1,0:T(8,128)S(1)}, f32[33,31,1536]{2,1,0:T(8,128)}, u32[]{:S(2)}) copy-start(f32[33,31,1536]{2,1,0:T(8,128)} %squeeze.62) | copy-start | bytes 18855940
  190.1 9.6 %copy-start.3 = (f32[33,31,1536]{2,1,0:T(8,128)S(1)}, f32[33,31,1536]{2,1,0:T(8,128)}, u32[]{:S(2)}) copy-start(f32[33,31,1536]{2,1,0:T(8,128)} %squeeze.63) | copy-start | bytes 18855940
  372.6 54.5 %copy-start.4 = (f32[1,31,33]{2,0,1:T(1,128)}, f32[1,31,33]{2,0,1:T(1,128)S(1)}, u32[]{:S(2)}) copy-start(f32[1,31,33]{2,0,1:T(1,128)S(1)} %broadcast_select_fusion.55) | copy-start | bytes 12280
  452.1 8.1 %slice-start.2 = ((f32[1,31,33]{2,0,1:T(1,128)}), f32[1,28,33]{2,0,1:T(1,128)S(1)}, s32[]{:S(2)}) async-start(f32[1,31,33]{2,0,1:T(1,128)} %copy-done.4), calls=%async_computation.4 | async-start | bytes 28672 | tf_op jit(solution)/shard_map/slice | solution.py:82
  466.4 9.6 %copy-start.5 = (f32[31,31,33]{0,1,2:T(8,128)}, f32[31,31,33]{0,1,2:T(8,128)S(1)}, u32[]{:S(2)}) copy-start(f32[31,31,33]{0,1,2:T(8,128)S(1)} %copy.17831) | copy-start | bytes 380560
  476.8 10.2 %slice-start = ((s8[6488064]{0:T(1024)(128)(4,1)}), s8[2293760]{0:T(1024)(128)(4,1)S(1)}, s32[]{:S(2)}) async-start(s8[6488064]{0:T(1024)(128)(4,1)} %bitcast.637), calls=%async_computation.2 | async-start | bytes 4587520
  477.4 9.6 %slice-start.1 = ((s8[6488064]{0:T(1024)(128)(4,1)}), s8[4194304]{0:T(1024)(128)(4,1)S(1)}, s32[]{:S(2)}) async-start(s8[6488064]{0:T(1024)(128)(4,1)} %bitcast.637), calls=%async_computation.3 | async-start | bytes 8388608
  520.0 15.3 %copy-start.1 = (f32[16]{0:T(128)S(1)}, f32[16]{0:T(128)}, u32[]{:S(2)}) copy-start(f32[16]{0:T(128)} %param.7) | copy-start | bytes 196
Sparse Core Ops, SparseCore 0:
  222.0 147.0 all-reduce.3
where the time goes:
time: 550 us; the launch traced here: 543 us
  local copies, waits for them, and re-layouts  208 us (38%)
  waiting for transfers between devices  193 us (35%)
  matrix products  77.5 us (14%)
  other arithmetic  36.1 us (7%)
  between operations  19.5 us (4%)
  starting transfers between devices  8.64 us (2%)
    psum x1, waiting for transfers between devices, on_device(): sum_real, sum_imag = lax.psum((part_real, part_imag), ('pts', 'snap'))  147 us
    unnamed x352, local copies, waits for them, and re-layouts  52.7 us
    all_to_all x1, waiting for transfers between devices, on_device(): lax.all_to_all(snapshots, 'snap', split_axis=2, concat_axis=0, tiled=True)  45.5 us
    slice x3, local copies, waits for them, and re-layouts, gram(): amp_real, amp_imag = (amplitude[0], amplitude[1])  33.9 us
    squeeze x2, local copies, waits for them, and re-layouts, gram(): amp_real, amp_imag = (amplitude[0], amplitude[1])  23 us
    another operation x2, local copies, waits for them, and re-layouts, project(): return jnp.stack([mode_real, mode_imag])  14.5 us
    all_to_all x2, local copies, waits for them, and re-layouts, on_device(): lax.all_to_all(snapshots, 'snap', split_axis=2, concat_axis=0, tiled=True)  13 us
    another operation x27, local copies, waits for them, and re-layouts, complex_cholesky(): done_real = jnp.stack(rows_real)  11.6 us
  transfers between devices with their start and end apart: 2, of which 2 were waited for; matrix products, arithmetic and copies ran while one was open for 0% of the time, Pallas kernels for 0%

commit v1 on v0

--- a/solution.py
+++ b/solution.py
@@ -106,7 +106,12 @@
 
 def on_device(snapshots, block_starts, point_slab, slab_weight):
     dft_table, row_sums = make_tables(WIN, WIN // 2 + 1)
-    series = lax.all_to_all(snapshots, "snap", split_axis=2, concat_axis=0, tiled=True)
+    series = jnp.concatenate(
+        lax.all_to_all(
+            jnp.stack(jnp.split(snapshots, lax.axis_size("snap"), axis=2)), "snap", 0, 0
+        ),
+        axis=0,
+    )
     spectrum = spectra(series, block_starts, dft_table, row_sums)
     freq_count = spectrum.shape[1]
     block_count = spectrum.shape[2]

time: 550 us -> 530 us (0.964)
  local copies, waits for them, and re-layouts: 208 us -> 192 us
    unnamed x352 -> x368, local copies, waits for them, and re-layouts: 52.7 us -> 43.1 us
    all_to_all x2 -> x1, local copies, waits for them, and re-layouts: 13 us -> 4.73 us  [on_device(): lax.all_to_all(jnp.stack(jnp.split(snapshots, lax.axis_size('snap'), axis...]
where the time goes in v1:
time: 530 us; the launch traced here: 525 us
  waiting for transfers between devices  193 us (36%)
  local copies, waits for them, and re-layouts  192 us (36%)
  matrix products  75.5 us (14%)
  other arithmetic  36.6 us (7%)
  between operations  19.5 us (4%)
  starting transfers between devices  8.64 us (2%)
    psum x1, waiting for transfers between devices, on_device(): sum_real, sum_imag = lax.psum((part_real, part_imag), ('pts', 'snap'))  147 us
    all_to_all x1, waiting for transfers between devices, on_device(): lax.all_to_all(jnp.stack(jnp.split(snapshots, lax.axis_size('snap'), axis...  45.5 us
    unnamed x368, local copies, waits for them, and re-layouts  43.1 us
    slice x3, local copies, waits for them, and re-layouts, gram(): amp_real, amp_imag = (amplitude[0], amplitude[1])  33.9 us
    squeeze x2, local copies, waits for them, and re-layouts, gram(): amp_real, amp_imag = (amplitude[0], amplitude[1])  23 us
    another operation x2, local copies, waits for them, and re-layouts, project(): return jnp.stack([mode_real, mode_imag])  14.5 us
    another operation x27, local copies, waits for them, and re-layouts, complex_cholesky(): done_real = jnp.stack(rows_real)  11.6 us
    gather x1, local copies, waits for them, and re-layouts, spectra(): lax.dynamic_slice_in_dim(series, offset, WIN, 0)  11.6 us
  transfers between devices with their start and end apart: 2, of which 2 were waited for; matrix products, arithmetic and copies ran while one was open for 0% of the time, Pallas kernels for 0%

profile of v1, /device:TPU:1, one launch (start us, length us, event | category | flops | bytes accessed | tf_op | source)
XLA Modules:
  0.0 524.9 jit_solution(7392210767307836956)
XLA Ops:
  7.2 1.6 constant_dynamic-update-slice_fusion.15
  8.8 1.6 constant_dynamic-update-slice_fusion.14
  10.4 1.6 constant_dynamic-update-slice_fusion.13
  12.0 1.6 constant_dynamic-update-slice_fusion.12
  13.7 1.6 constant_dynamic-update-slice_fusion.11
  15.3 1.6 constant_dynamic-update-slice_fusion.10
  16.9 1.6 constant_dynamic-update-slice_fusion.9
  18.5 1.6 constant_dynamic-update-slice_fusion.8
  20.1 1.6 constant_dynamic-update-slice_fusion.7
  21.7 1.6 constant_dynamic-update-slice_fusion.6
  23.3 1.6 constant_dynamic-update-slice_fusion.5
  25.0 1.6 constant_dynamic-update-slice_fusion.4
  26.6 1.6 constant_dynamic-update-slice_fusion.3
  28.2 1.6 constant_dynamic-update-slice_fusion.2
  29.8 1.6 constant_dynamic-update-slice_fusion.1
  31.4 1.6 constant_dynamic-update-slice_fusion
  33.1 8.6 %all-to-all-start = ((bf16[16,64,3,512]{3,1,2,0:T(8,128)(2,1)}), bf16[16,64,3,512]{3,1,2,0:T(8,128)(2,1)S(1)}, u32[]{:S(2)}, u32[]{:S(2)}) async-start(bf16[16,64,3,512]{3,1,2,0:T(8,128)(2,1)} %constant_dynamic-update-slice_fusion), calls=%async_computation | async-start | bytes 6291456 | tf_op jit(solution)/shard_map/all_to_all | solution.py:110
  42.8 45.5 %all-to-all-done = bf16[16,64,3,512]{3,1,2,0:T(8,128)(2,1)S(1)} async-done(((bf16[16,64,3,512]{3,1,2,0:T(8,128)(2,1)}), bf16[16,64,3,512]{3,1,2,0:T(8,128)(2,1)S(1)}, u32[]{:S(2)}, u32[]{:S(2)}) %all-to-all-start) | async-done | bytes 3145760 | tf_op jit(solution)/shard_map/all_to_all | solution.py:110
  88.8 0.9 broadcast_multiply_fusion.2
  89.7 4.7 copy.17230
  94.4 11.6 %gather_fusion = bf16[31,64,3,512]{3,2,1,0:T(4,128)(2,1)} fusion(bf16[1024,3,512]{2,1,0:T(4,128)(2,1)} %bitcast.662, s32[31]{0:T(128)S(1)} %fusion.108), kind=kCustom, calls=%fused_computation | custom fusion | bytes 12190068 | tf_op jit(solution)/shard_map/vmap()/gather | solution.py:25
  106.0 11.4 %subtract_multiply_fusion = f32[2,33,31,3,512]{4,1,3,2,0:T(8,128)} fusion(f32[512]{0:T(512)S(1)} %multiply_sqrt_fusion, f32[2,33,3,512]{3,1,2,0:T(8,128)S(1)} %copy-done.7, bf16[31,64,3,512]{3,2,1,0:T(4,128)(2,1)} %gather_fusion, bf16[1,33,64]{2,1,0:T(8,128)(2,1)S(1)} %get-tuple-element.379, bf16[1,33,64]{2,1,0:T(8,128)(2,1)S(1)} %get-tuple-element.380), kind=kOutput, calls=%fused_computation.1 | convolution fusion | flops 408562176 | bytes 19081472 | tf_op jit(solution)/shard_map/kfw,bwcp->kfbcp/dot_general | solution.py:26
  117.5 12.5 %fusion.116 = (f32[1,33,31,3,512]{4,1,3,2,0:T(8,128)}, f32[1,33,31,3,512]{4,1,3,2,0:T(8,128)}) fusion(f32[2,33,31,3,512]{4,1,3,2,0:T(8,128)} %subtract_multiply_fusion), kind=kLoop, calls=%fused_computation.944 | loop fusion | bytes 25141248 | tf_op jit(solution)/shard_map/slice | solution.py:33
  130.0 10.7 %copy.17232 = f32[1,33,31,3,512]{4,3,2,1,0:T(4,128)} copy(f32[1,33,31,3,512]{4,1,3,2,0:T(8,128)} %get-tuple-element.190) | data formatting | bytes 12570624 | tf_op jit(solution)/shard_map/slice | solution.py:33
  140.7 11.6 %squeeze.62 = f32[33,31,1536]{2,1,0:T(8,128)} reshape(f32[1,33,31,3,512]{4,3,2,1,0:T(4,128)} %copy.17232) | data formatting | bytes 12570624 | tf_op jit(solution)/shard_map/squeeze | solution.py:33
  152.3 10.7 %copy.17233 = f32[1,33,31,3,512]{4,3,2,1,0:T(4,128)} copy(f32[1,33,31,3,512]{4,1,3,2,0:T(8,128)} %get-tuple-element.191) | data formatting | bytes 12570624 | tf_op jit(solution)/shard_map/slice | solution.py:33
  163.0 11.4 %squeeze.63 = f32[33,31,1536]{2,1,0:T(8,128)} reshape(f32[1,33,31,3,512]{4,3,2,1,0:T(4,128)} %copy.17233) | data formatting | bytes 12570624 | tf_op jit(solution)/shard_map/squeeze | solution.py:33
  174.4 9.6 %fusion.123 = f32[33,31,31]{2,1,0:T(8,128)S(1)} fusion(f32[33,31,1536]{2,1,0:T(8,128)} %squeeze.62, f32[33,31,1536]{2,1,0:T(8,128)} %squeeze.63), kind=kOutput, calls=%fused_computation.951 | convolution fusion | flops 584534016 | bytes 12697476 | tf_op jit(solution)/shard_map/fbn,fdn->bdf/dot_general | solution.py:37
  184.0 6.0 %fusion.122 = f32[33,31,31]{2,1,0:T(8,128)S(1)} fusion(f32[33,31,1536]{2,1,0:T(8,128)S(1)} %copy-done.3, f32[33,31,1536]{2,1,0:T(8,128)S(1)} %copy-done.2), kind=kOutput, calls=%fused_computation.950 | convolution fusion | flops 584534016 | bytes 12697476 | tf_op jit(solution)/shard_map/fbn,fdn->bdf/dot_general | solution.py:37
  190.0 6.3 %fusion.120 = f32[33,31,31]{2,1,0:T(8,128)S(1)} fusion(f32[33,31,1536]{2,1,0:T(8,128)S(1)} %copy-done.2), kind=kOutput, calls=%fused_computation.948 | convolution fusion | flops 584534016 | bytes 6412164 | tf_op jit(solution)/shard_map/fbn,fdn->bdf/dot_general | solution.py:34
  196.4 6.1 %fusion.121 = f32[33,31,31]{2,1,0:T(8,128)S(1)} fusion(f32[33,31,1536]{2,1,0:T(8,128)S(1)} %copy-done.3), kind=kOutput, calls=%fused_computation.949 | convolution fusion | flops 584534016 | bytes 6412164 | tf_op jit(solution)/shard_map/fbn,fdn->bdf/dot_general | solution.py:34
  204.4 0.9 subtract_bitcast_fusion
  205.3 0.9 add_bitcast_fusion
  206.2 147.2 %all-reduce.4.cloned.1.call-done = (f32[31,31,33]{2,0,1:T(8,128)}, f32[31,31,33]{2,0,1:T(8,128)}) async-done(((f32[31,31,33]{2,0,1:T(8,128)}, f32[31,31,33]{2,0,1:T(8,128)}), (f32[31,31,33]{2,0,1:T(8,128)}, f32[31,31,33]{2,0,1:T(8,128)})) %all-reduce.4.cloned.1.call-update) | async-done | bytes 253720 | tf_op jit(solution)/shard_map/psum | solution.py:127
  353.4 1.1 broadcast_multiply_fusion.1
  354.5 1.1 broadcast_multiply_fusion
  379.9 0.8 stack.343
  412.1 1.0 copy.17836
  413.3 2.0 copy.17838
  445.1 0.9 stack.426
  450.7 9.6 %fusion.124 = f32[33,31,1536]{2,1,0:T(8,128)} fusion(f32[31,31,33]{0,1,2:T(8,128)S(1)} %copy.17825, f32[33,31,1536]{2,1,0:T(8,128)} %squeeze.62), kind=kOutput, calls=%fused_computation.952 | convolution fusion | flops 584534016 | bytes 12697476 | tf_op jit(solution)/shard_map/fbn,bmf->fmn/dot_general | solution.py:98
  461.7 9.6 %fusion.125 = f32[33,31,1536]{2,1,0:T(8,128)} fusion(f32[31,31,33]{0,1,2:T(8,128)S(1)} %copy.17829, f32[33,31,1536]{2,1,0:T(8,128)} %squeeze.62), kind=kOutput, calls=%fused_computation.953 | convolution fusion | flops 584534016 | bytes 12697476 | tf_op jit(solution)/shard_map/fbn,bmf->fmn/dot_general | solution.py:101
  471.3 7.6 %subtract_convert_fusion = bf16[33,31,1536]{2,1,0:T(8,128)(2,1)} fusion(f32[33,31,1536]{2,1,0:T(8,128)S(1)} %copy-done.4, f32[31,31,33]{0,1,2:T(8,128)S(1)} %copy.17829, f32[33,31,1536]{2,1,0:T(8,128)S(1)} %bitcast.661), kind=kOutput, calls=%fused_computation.4 | convolution fusion | flops 587676672 | bytes 15840132 | tf_op jit(solution)/shard_map/fbn,bmf->fmn/dot_general | solution.py:98
  478.9 8.7 %stack.431 = bf16[1,33,31,3,512]{4,3,2,1,0:T(4,128)(2,1)} reshape(bf16[33,31,1536]{2,1,0:T(8,128)(2,1)} %subtract_convert_fusion) | data formatting | bytes 6285312 | tf_op jit(solution)/shard_map/stack | solution.py:104
  487.6 8.9 %add_convert_fusion = bf16[33,31,1536]{2,1,0:T(8,128)(2,1)S(1)} fusion(f32[33,31,1536]{2,1,0:T(8,128)} %fusion.125, f32[31,31,33]{0,1,2:T(8,128)} %copy-done.6, f32[33,31,1536]{2,1,0:T(8,128)} %squeeze.63), kind=kOutput, calls=%fused_computation.3 | convolution fusion | flops 587676672 | bytes 15840132 | tf_op jit(solution)/shard_map/fbn,bmf->fmn/dot_general | solution.py:101
  496.6 5.8 %stack.432 = bf16[1,33,31,3,512]{4,3,2,1,0:T(4,128)(2,1)} reshape(bf16[33,31,1536]{2,1,0:T(8,128)(2,1)S(1)} %add_convert_fusion) | data formatting | bytes 6285312 | tf_op jit(solution)/shard_map/stack | solution.py:104
  502.4 7.6 %pad_maximum_fusion = bf16[2,33,31,3,512]{4,3,2,1,0:T(4,128)(2,1)S(1)} fusion(bf16[1,33,31,3,512]{4,3,2,1,0:T(4,128)(2,1)} %stack.432, bf16[1,33,31,3,512]{4,3,2,1,0:T(4,128)(2,1)} %stack.431), kind=kLoop, calls=%fused_computation.2 | loop fusion | flops 3142656 | bytes 12570624 | tf_op jit(solution)/shard_map/stack | solution.py:104
  510.0 7.6 %copy.17837 = bf16[2,33,31,3,512]{4,0,3,2,1:T(2,128)(2,1)} copy(bf16[2,33,31,3,512]{4,3,2,1,0:T(4,128)(2,1)S(1)} %pad_maximum_fusion) | data formatting | bytes 12570624
  (970 shorter events, 90.5 us)
Async XLA Ops:
  7.2 35.2 %copy-start = (f32[16]{0:T(128)S(1)}, f32[16]{0:T(128)}, u32[]{:S(2)}) copy-start(f32[16]{0:T(128)} %param.7) | copy-start | bytes 196
  25.0 17.4 %copy-start.9 = (s32[31]{0:T(128)S(1)}, s32[31]{0:T(128)}, u32[]{:S(2)}) copy-start(s32[31]{0:T(128)} %param.5) | copy-start | bytes 376
  25.0 17.4 %copy-start.8 = (s32[512]{0:T(512)S(1)}, s32[512]{0:T(512)}, u32[]{:S(2)}) copy-start(s32[512]{0:T(512)} %param.6) | copy-start | bytes 6148
  33.1 55.2 %all-to-all-start = ((bf16[16,64,3,512]{3,1,2,0:T(8,128)(2,1)}), bf16[16,64,3,512]{3,1,2,0:T(8,128)(2,1)S(1)}, u32[]{:S(2)}, u32[]{:S(2)}) async-start(bf16[16,64,3,512]{3,1,2,0:T(8,128)(2,1)} %constant_dynamic-update-slice_fusion), calls=%async_computation | async-start | bytes 6291456 | tf_op jit(solution)/shard_map/all_to_all | solution.py:110
  41.7 311.7 %all-reduce.4.cloned.1.call-start = ((), (), s32[]{:S(2)}) async-start(), calls=%async_computation.1 | async-start | bytes 2031616 | tf_op jit(solution)/shard_map/psum | solution.py:127
  94.4 11.6 %copy-start.7 = (f32[2,33,3,512]{3,1,2,0:T(8,128)S(1)}, f32[2,33,3,512]{3,1,2,0:T(8,128)}, u32[]{:S(2)}) copy-start(f32[2,33,3,512]{3,1,2,0:T(8,128)} %broadcast_multiply_fusion.2) | copy-start | bytes 1216516
  174.4 9.6 %copy-start.2 = (f32[33,31,1536]{2,1,0:T(8,128)S(1)}, f32[33,31,1536]{2,1,0:T(8,128)}, u32[]{:S(2)}) copy-start(f32[33,31,1536]{2,1,0:T(8,128)} %squeeze.62) | copy-start | bytes 18855940
  174.4 9.6 %copy-start.3 = (f32[33,31,1536]{2,1,0:T(8,128)S(1)}, f32[33,31,1536]{2,1,0:T(8,128)}, u32[]{:S(2)}) copy-start(f32[33,31,1536]{2,1,0:T(8,128)} %squeeze.63) | copy-start | bytes 18855940
  356.8 54.5 %copy-start.5 = (f32[1,31,33]{2,0,1:T(1,128)}, f32[1,31,33]{2,0,1:T(1,128)S(1)}, u32[]{:S(2)}) copy-start(f32[1,31,33]{2,0,1:T(1,128)S(1)} %broadcast_select_fusion.55) | copy-start | bytes 12280
  439.2 5.3 %slice-start.2 = ((f32[1,31,33]{2,0,1:T(1,128)}), f32[1,28,33]{2,0,1:T(1,128)S(1)}, s32[]{:S(2)}) async-start(f32[1,31,33]{2,0,1:T(1,128)} %copy-done.5), calls=%async_computation.4 | async-start | bytes 28672 | tf_op jit(solution)/shard_map/slice | solution.py:82
  450.7 9.6 %copy-start.6 = (f32[31,31,33]{0,1,2:T(8,128)}, f32[31,31,33]{0,1,2:T(8,128)S(1)}, u32[]{:S(2)}) copy-start(f32[31,31,33]{0,1,2:T(8,128)S(1)} %copy.17825) | copy-start | bytes 380560
  461.1 10.2 %slice-start = ((s8[6488064]{0:T(1024)(128)(4,1)}), s8[2293760]{0:T(1024)(128)(4,1)S(1)}, s32[]{:S(2)}) async-start(s8[6488064]{0:T(1024)(128)(4,1)} %bitcast.660), calls=%async_computation.2 | async-start | bytes 4587520
  461.7 9.6 %slice-start.1 = ((s8[6488064]{0:T(1024)(128)(4,1)}), s8[4194304]{0:T(1024)(128)(4,1)S(1)}, s32[]{:S(2)}) async-start(s8[6488064]{0:T(1024)(128)(4,1)} %bitcast.660), calls=%async_computation.3 | async-start | bytes 8388608
  461.7 9.6 %copy-start.4 = (f32[33,31,1536]{2,1,0:T(8,128)S(1)}, f32[33,31,1536]{2,1,0:T(8,128)}, u32[]{:S(2)}) copy-start(f32[33,31,1536]{2,1,0:T(8,128)} %fusion.124) | copy-start | bytes 18855940
  502.4 15.3 %copy-start.1 = (f32[16]{0:T(128)S(1)}, f32[16]{0:T(128)}, u32[]{:S(2)}) copy-start(f32[16]{0:T(128)} %param.7) | copy-start | bytes 196
Sparse Core Ops, SparseCore 0:
  206.3 147.0 all-reduce.3
